TPU v7x, 128 devices: a whole 4x4x4 slice. The times are simulated.
128 devices in a mesh: role: 2 (over core), seq: 16 (over z, x), tp: 4 (over y).
Axes of the slice: x: 4, y: 4, z: 4, core: 2. Of those that a mesh axis runs over, the one named last changes fastest.
Arguments:
- merger_hidden: bfloat16 [2048, 5120], P(('role', 'seq'), 'tp'), may hold values from -6 to 6
- merger_out: bfloat16 [5120, 8192], P('tp', ('role', 'seq')), may hold values from -0.078125 to 0.078125
- row_position: int32 [2048], P(('role', 'seq')), may hold values from -1 to 8191, as said below
- prompt_embeds: bfloat16 [8192, 8192], P(('role', 'seq'), 'tp'), may hold values from -300 to 300
- norm_gain: bfloat16 [8192], P('tp'), may hold values from 0.099609375 to 1.8984375
- query_weight: bfloat16 [8192, 4096], P(None, 'tp'), may hold values from -2.762136 to 2.762136
- key_weight: bfloat16 [8192, 512], P(None, 'tp'), may hold values from -0.06629126 to 0.06629126
- value_weight: bfloat16 [8192, 512], P(None, 'tp'), may hold values from -0.0625 to 0.0625
Outputs:
- stream: bfloat16 [8192, 8192], P(('role', 'seq'), 'tp')
- context: bfloat16 [8192, 4096], P(('role', 'seq'), 'tp')
Inputs may be any that keep to these rules, and one draw needn't show every extreme that they name: `row_position`: the live slots of each device's 64 come first and hold distinct prompt positions, distinct over all devices; the other slots hold -1. Of one device's slots at most 4 hold positions of one owner's block (positions j * 256 to (j + 1) * 256 - 1); every device has 4 or more live slots.
All inputs are finite; a program needn't handle non-finite values.
Results may differ from a plain program's by a relative error of at most 0.012.
The roundings to bfloat16 on the way count: a program that leaves them out, or rounds other values in their place, can miss the bound.
Values may be sent and summed in bfloat16 or wider, within the bound.
A program may use at most 192 MiB of HBM per device.

v0:
```python
import math
import jax
import jax.numpy as jnp
from jax import lax
from jax.sharding import PartitionSpec as P

HEAD_DIM = 128


def split_up(x, dim, length):
    before, after = (x.shape[:dim], x.shape[dim + 1 :])
    return jnp.moveaxis(x.reshape(*before, length, -1, *after), dim, 0)


def in_order(blocks, dim):
    lengths = list(blocks.shape[1:])
    lengths[dim] *= blocks.shape[0]
    return jnp.moveaxis(blocks, 0, dim).reshape(lengths)


def exchange_both(x, axis, axes, splits, concats):
    sizes = [lax.axis_size(a) for a in axes]
    blocks = split_up(x, splits[0], sizes[0])
    blocks = jnp.moveaxis(split_up(blocks, splits[1] + 1, sizes[1]), 0, 1)
    inside = blocks.shape[2:]
    blocks = blocks.reshape(-1, *inside)
    blocks = lax.all_to_all(blocks, axis, split_axis=0, concat_axis=0, tiled=True)
    blocks = in_order(blocks.reshape(*sizes, *inside), concats[0] + 1)
    return in_order(blocks, concats[1])


def sent_together(arrays, axis, dim, along):
    widths = [a.shape[along] for a in arrays]
    both = jnp.concatenate(arrays, axis=along)
    filled = lax.all_gather(both, axis, axis=dim, tiled=True)
    return tuple(jnp.split(filled, [sum(widths[:k]) for k in range(1, len(widths))], axis=along))


def rotate(vectors, positions):
    half_dim = vectors.shape[-1] // 2
    frequency = 1000000.0 ** (-jnp.arange(half_dim, dtype=jnp.float32) / half_dim)
    angles = positions.astype(jnp.float32)[:, None, None] * frequency[None, None, :]
    cosine = jnp.cos(angles)
    sine_part = jnp.sin(angles)
    lower_half = vectors[..., :half_dim]
    upper_half = vectors[..., half_dim:]
    return jnp.concatenate(
        [
            lower_half * cosine - upper_half * sine_part,
            upper_half * cosine + lower_half * sine_part,
        ],
        axis=-1,
    )


def sum_hidden(partial_value):
    return lax.psum_scatter(partial_value, "tp", scatter_dimension=1, tiled=True).astype(
        jnp.bfloat16
    )


def project_strips(merger_hidden, merger_out):
    return jnp.dot(
        lax.all_gather(merger_hidden, ("role", "seq"), axis=0, tiled=True),
        merger_out,
        preferred_element_type=jnp.float32,
    )


def body(
    merger_hidden,
    merger_out,
    row_position,
    prompt_embeds,
    norm_gain,
    query_weight,
    key_weight,
    value_weight,
):
    groups = lax.axis_size("role") * lax.axis_size("seq")
    device_rank = lax.axis_index(("role", "seq"))
    row_count = merger_hidden.shape[0]
    tok_count = prompt_embeds.shape[0]
    columns = prompt_embeds.shape[1]
    model_width = columns * lax.axis_size("tp")
    capacity = 2 * row_count // groups
    strips = project_strips(merger_hidden, merger_out)
    partial_value = lax.all_to_all(strips, ("role", "seq"), split_axis=0, concat_axis=1, tiled=True)
    embeds = sum_hidden(partial_value)
    owners = jnp.where(row_position >= 0, row_position // tok_count, groups)
    onehot = (owners[:, None] == jnp.arange(groups, dtype=jnp.int32)[None, :]).astype(jnp.int32)
    earlier = jnp.sum((jnp.cumsum(onehot, axis=0) - onehot) * onehot, axis=1)
    buffer_slot = jnp.where(owners < groups, owners * capacity + earlier, groups * capacity)
    source = (
        jnp.full((groups * capacity,), row_count, jnp.int32)
        .at[buffer_slot]
        .set(jnp.arange(row_count, dtype=jnp.int32), mode="drop")
    )
    padded = jnp.concatenate([embeds, jnp.zeros((1, columns), jnp.bfloat16)], axis=0)
    outgoing = padded[source].reshape(groups, capacity, columns)
    outgoing_pos = jnp.concatenate([row_position, jnp.full((1,), -1, jnp.int32)])[source].reshape(
        groups, capacity
    )
    role_count = lax.axis_size("role")
    seq_count = lax.axis_size("seq")
    arrived, arrived_pos = (
        exchange_both(
            outgoing.reshape(role_count, seq_count, capacity, columns),
            ("role", "seq"),
            ("role", "seq"),
            (0, 1),
            (0, 1),
        ),
        exchange_both(
            outgoing_pos.reshape(role_count, seq_count, capacity),
            ("role", "seq"),
            ("role", "seq"),
            (0, 1),
            (0, 1),
        ),
    )
    arrived_pos = arrived_pos.reshape(-1)
    local_row = jnp.where(arrived_pos >= 0, arrived_pos - device_rank * tok_count, tok_count)
    stream = prompt_embeds.at[local_row].set(arrived.reshape(-1, columns), mode="drop")
    widened = stream.astype(jnp.float32)
    squares = lax.psum(jnp.sum(widened * widened, axis=1), "tp")
    inverse = lax.rsqrt(squares / model_width + 1e-06)[:, None]
    normed = (widened * inverse * norm_gain.astype(jnp.float32)[None, :]).astype(jnp.bfloat16)
    tables = (query_weight, key_weight, value_weight)
    shard_piece = lax.all_gather(normed, "tp", axis=1, tiled=True)
    query_sum, key_sum, value_sum = tuple(
        (jnp.dot(shard_piece, table, preferred_element_type=jnp.float32) for table in tables)
    )
    local_heads = query_weight.shape[1] // HEAD_DIM
    local_kv = key_weight.shape[1] // HEAD_DIM
    group_size = local_heads // local_kv
    positions = device_rank * tok_count + jnp.arange(tok_count, dtype=jnp.int32)
    queries = rotate(query_sum.reshape(tok_count, local_heads, HEAD_DIM), positions).astype(
        jnp.bfloat16
    )
    queries = queries.reshape(tok_count, local_kv, group_size, HEAD_DIM)
    key_rows = rotate(key_sum.reshape(tok_count, local_kv, HEAD_DIM), positions).astype(
        jnp.bfloat16
    )
    value_rows = value_sum.astype(jnp.bfloat16).reshape(tok_count, local_kv, HEAD_DIM)
    score_scale = 1.0 / math.sqrt(HEAD_DIM)
    running_max = jnp.full((local_kv, group_size, tok_count), -1e30, jnp.float32)
    key_piece, value_piece = sent_together((key_rows, value_rows), ("role", "seq"), 0, 1)
    scores = (
        jnp.einsum("qhgd,khd->hgqk", queries, key_piece, preferred_element_type=jnp.float32)
        * score_scale
    )
    key_pos = jnp.arange(key_piece.shape[0], dtype=jnp.int32)
    visible = key_pos[None, :] <= positions[:, None]
    scores = jnp.where(visible, scores, -jnp.inf)
    next_max = jnp.maximum(running_max, jnp.max(scores, axis=3))
    probability = jnp.where(visible, jnp.exp(scores - next_max[..., None]), 0.0)
    running_sum = jnp.sum(probability, axis=3)
    running_out = jnp.einsum(
        "hgqk,khd->hgqd",
        probability.astype(jnp.bfloat16),
        value_piece,
        preferred_element_type=jnp.float32,
    )
    running_max, running_sum, running_out = (next_max, running_sum, running_out)
    context = running_out / running_sum[..., None]
    context = (
        jnp.transpose(context, (2, 0, 1, 3))
        .reshape(tok_count, local_heads * HEAD_DIM)
        .astype(jnp.bfloat16)
    )
    return (stream, context)


def solution(mesh):
    in_specs = (
        P(("role", "seq"), "tp"),
        P("tp", ("role", "seq")),
        P(("role", "seq")),
        P(("role", "seq"), "tp"),
        P("tp"),
        P(None, "tp"),
        P(None, "tp"),
        P(None, "tp"),
    )
    out_specs = (P(("role", "seq"), "tp"), P(("role", "seq"), "tp"))
    return jax.shard_map(body, mesh=mesh, in_specs=in_specs, out_specs=out_specs, check_vma=False)
```

profile of v0, /device:TPU:1, one launch (start us, length us, event | category | flops | bytes accessed | tf_op | source)
XLA Modules:
  0.0 347.9 jit_solution(12780545009831213138)
XLA Ops:
  7.2 0.0 all-gather.4.cloned.1.call-start
  7.2 0.7 all-gather.4.cloned.1.call-update
  7.9 0.0 reduce-scatter.2.cloned.1.call-start
  8.0 53.5 %all-gather.4.cloned.1.call-done = bf16[2048,1280]{1,0:T(8,128)(2,1)} async-done(((bf16[64,1280]{1,0:T(8,128)(2,1)}), bf16[2048,1280]{1,0:T(8,128)(2,1)}) %all-gather.4.cloned.1.call-update) | async-done | bytes 5242896 | tf_op jit(solution)/shard_map/all_gather | solution.py:64
  61.5 4.2 %fusion.35 = f32[2048,256]{1,0:T(8,128)S(1)} fusion(bf16[2048,1280]{1,0:T(8,128)(2,1)} %all-gather.4.cloned.1.call-done, bf16[1280,256]{1,0:T(8,128)(2,1)} %param.9), kind=kOutput, calls=%fused_computation.73 | convolution fusion | flops 1342177280 | bytes 7995392 | tf_op jit(solution)/shard_map/dot_general | solution.py:63
  65.7 32.9 %all_to_all.29 = f32[32,64,256]{2,1,0:T(8,128)S(1)} all-to-all(f32[32,64,256]{2,1,0:T(8,128)S(1)} %bitcast.88), channel_id=1, replica_groups=mesh['role'=2,'seq'=16,'tp'=4] {'role','seq'}, dimensions={0} | all-to-all | bytes 4194304 | tf_op jit(solution)/shard_map/all_to_all | solution.py:88
  98.5 1.5 copy.49
  100.0 0.0 reduce-scatter.2.cloned.1.call-update
  100.1 0.1 fusion.25
  100.2 0.1 reduce_window_sum.11
  100.3 0.2 select_reduce_fusion
  100.5 0.8 scatter_custom_fusion
  101.3 0.1 pad_add_fusion
  101.4 1.2 gather_fusion
  102.6 0.7 reshape_transpose_transpose_reshape_reshape_reshape_reshape.6
  103.3 5.1 %all-to-all-start = ((s32[32,1,1,4]{3,2,1,0:T(1,128)}), s32[32,1,1,4]{3,2,1,0:T(1,128)S(1)}, u32[]{:S(2)}, u32[]{:S(2)}) async-start(s32[32,1,1,4]{3,2,1,0:T(1,128)} %bitcast), calls=%async_computation | async-start | bytes 32768 | tf_op jit(solution)/shard_map/all_to_all | solution.py:27
  108.4 19.6 %reduce-scatter.2.cloned.1.call-done = f32[64,2048]{1,0:T(8,128)} async-done(((f32[64,8192]{1,0:T(8,128)}), f32[64,2048]{1,0:T(8,128)}) %reduce-scatter.2.cloned.1.call-update) | async-done | bytes 524304 | tf_op jit(solution)/shard_map/reduce_scatter | solution.py:57
  128.0 1.1 convert_element_type.54
  129.1 1.7 gather_fusion.1
  130.8 2.0 reshape_transpose_transpose_reshape_reshape_reshape_reshape.7
  132.9 7.7 %all-to-all-start.2 = ((bf16[32,1,1,4,2048]{4,3,2,1,0:T(4,128)(2,1)}), bf16[32,1,1,4,2048]{4,3,2,1,0:T(4,128)(2,1)}, u32[]{:S(2)}, u32[]{:S(2)}) async-start(bf16[32,1,1,4,2048]{4,3,2,1,0:T(4,128)(2,1)} %bitcast.89), calls=%async_computation.3 | async-start | bytes 1048576 | tf_op jit(solution)/shard_map/all_to_all | solution.py:27
  140.5 0.0 all-gather.6.cloned.1.call-start
  140.6 0.1 copy.45
  140.7 0.1 copy.33
  140.8 0.1 select_n.64
  141.0 10.7 %all-to-all-done.2 = bf16[32,1,1,4,2048]{4,3,2,1,0:T(4,128)(2,1)} async-done(((bf16[32,1,1,4,2048]{4,3,2,1,0:T(4,128)(2,1)}), bf16[32,1,1,4,2048]{4,3,2,1,0:T(4,128)(2,1)}, u32[]{:S(2)}, u32[]{:S(2)}) %all-to-all-start.2) | async-done | bytes 524320 | tf_op jit(solution)/shard_map/all_to_all | solution.py:27
  151.7 2.0 reshape.301
  153.6 2.4 scatter_fusion
  156.1 0.3 fusion.7
  156.4 6.9 %psum.7 = f32[256]{0:T(256)S(1)} all-reduce(f32[256]{0:T(256)S(1)} %fusion.7), channel_id=1, replica_groups=mesh['role'=2,'seq'=16,'tp'=4] {'tp'}, use_global_device_ids=true, to_apply=%region_6.7 | all-reduce | flops 256 | bytes 2048 | tf_op jit(solution)/shard_map/psum | solution.py:126
  163.3 1.3 fusion.9
  164.6 0.0 all-gather.8.cloned.1.call-start
  164.7 45.9 %all-gather.6.cloned.1.call-done = bf16[256,8192]{1,0:T(8,128)(2,1)} async-done(((bf16[256,2048]{1,0:T(8,128)(2,1)}), bf16[256,8192]{1,0:T(8,128)(2,1)}) %all-gather.6.cloned.1.call-update) | async-done | bytes 4194320 | tf_op jit(solution)/shard_map/all_gather | solution.py:130
  210.6 3.8 %convolution_bitcast_fusion.1 = f32[256,1,128]{0,2,1:T(8,128)S(1)} fusion(bf16[256,8192]{1,0:T(8,128)(2,1)} %all-gather.6.cloned.1.call-done, bf16[8192,128]{1,0:T(8,128)(2,1)S(1)} %copy-done), kind=kOutput, calls=%fused_computation.22 | convolution fusion | flops 536870912 | bytes 6422528 | tf_op jit(solution)/shard_map/dot_general | solution.py:132
  214.5 0.3 fusion.22
  214.8 1.5 fusion.11
  216.3 0.7 pad_maximum_fusion
  217.0 0.5 multiply_cosine_fusion
  217.6 2.7 iota_compare_fusion
  220.3 9.5 %convolution_bitcast_fusion = f32[32,8,8,128]{3,1,2,0:T(8,128)S(1)} fusion(bf16[256,8192]{1,0:T(8,128)(2,1)} %all-gather.6.cloned.1.call-done, bf16[8192,1024]{1,0:T(8,128)(2,1)} %param.13), kind=kOutput, calls=%fused_computation.21 | convolution fusion | flops 4294967296 | bytes 22020096 | tf_op jit(solution)/shard_map/dot_general | solution.py:132
  229.8 0.2 copy.50
  230.0 0.3 fusion.34
  230.3 0.4 subtract_convert_fusion
  230.7 36.6 %all-gather.8.cloned.1.call-done = bf16[8192,2,128]{0,2,1:T(8,128)(2,1)} async-done(((bf16[256,2,128]{0,2,1:T(8,128)(2,1)}), bf16[8192,2,128]{0,2,1:T(8,128)(2,1)}) %all-gather.8.cloned.1.call-update) | async-done | bytes 4194320 | tf_op jit(solution)/shard_map/all_gather | solution.py:35
  267.3 25.4 %fusion = (f32[8,256]{1,0:T(8,128)S(1)}, f32[8192,256,8]{1,0,2:T(8,128)}) fusion(pred[256,8192]{0,1:T(8,128)(4,1)} %iota_compare_fusion, bf16[256,8,64]{2,0,1:T(8,128)(2,1)S(1)} %get-tuple-element.9, bf16[256,8,64]{2,0,1:T(8,128)(2,1)S(1)} %get-tuple-element.8, bf16[8192,2,128]{0,2,1:T(8,128)(2,1)} %all-gather.8.cloned.1.call-done), kind=kOutput, calls=%fused_computation.6 | convolution fusion | flops 4346345472 | bytes 71835648 | tf_op jit(solution)/shard_map/qhgd,khd->hgqk/dot_general | solution.py:150
  292.8 22.3 %fusion.1 = f32[8,256]{1,0:T(8,128)S(1)} fusion(f32[8192,256,8]{1,0,2:T(8,128)} %get-tuple-element.17, f32[8,256]{1,0:T(8,128)S(1)} %broadcast_maximum_fusion, pred[256,8192]{0,1:T(8,128)(4,1)} %iota_compare_fusion), kind=kLoop, calls=%fused_computation.7 | loop fusion | flops 83884032 | bytes 69222400 | tf_op jit(solution)/shard_map/reduce_sum | solution.py:158
  315.0 25.3 %divide_convert_fusion = bf16[8,256,128]{1,2,0:T(8,128)(2,1)S(1)} fusion(f32[8192,256,8]{1,0,2:T(8,128)} %get-tuple-element.17, f32[8,256]{1,0:T(8,128)S(1)} %broadcast_maximum_fusion, pred[256,8192]{0,1:T(8,128)(4,1)} %iota_compare_fusion, bf16[8192,2,128]{0,2,1:T(8,128)(2,1)} %all-gather.8.cloned.1.call-done, f32[8,256]{1,0:T(8,128)S(1)} %fusion.1), kind=kOutput, calls=%fused_computation.25 | convolution fusion | flops 4379377664 | bytes 71843840 | tf_op jit(solution)/shard_map/hgqk,khd->hgqd/dot_general | solution.py:159
  340.4 1.0 copy.41
  (32 shorter events, 0.2 us)
Async XLA Ops:
  7.2 203.4 %copy-start = (bf16[8192,128]{1,0:T(8,128)(2,1)S(1)}, bf16[8192,128]{1,0:T(8,128)(2,1)}, u32[]{:S(2)}) copy-start(bf16[8192,128]{1,0:T(8,128)(2,1)} %param.14) | copy-start | bytes 6291460
  7.2 54.3 %all-gather.4.cloned.1.call-start = ((), (), s32[]{:S(2)}) async-start(), calls=%async_computation.4 | async-start | bytes 5406720 | tf_op jit(solution)/shard_map/all_gather | solution.py:64
  7.9 120.1 %reduce-scatter.2.cloned.1.call-start = ((), (), s32[]{:S(2)}) async-start(), calls=%async_computation.5 | async-start | bytes 2621440 | tf_op jit(solution)/shard_map/reduce_scatter | solution.py:57
  98.5 1.5 copy-start.6
  102.6 38.0 %copy-start.5 = (bf16[2048]{0:T(1024)(128)(2,1)S(1)}, bf16[2048]{0:T(1024)(128)(2,1)}, u32[]{:S(2)}) copy-start(bf16[2048]{0:T(1024)(128)(2,1)} %param.12) | copy-start | bytes 12292
  103.3 29.5 %all-to-all-start = ((s32[32,1,1,4]{3,2,1,0:T(1,128)}), s32[32,1,1,4]{3,2,1,0:T(1,128)S(1)}, u32[]{:S(2)}, u32[]{:S(2)}) async-start(s32[32,1,1,4]{3,2,1,0:T(1,128)} %bitcast), calls=%async_computation | async-start | bytes 32768 | tf_op jit(solution)/shard_map/all_to_all | solution.py:27
  129.1 24.6 %copy-start.2 = (bf16[256,2048]{1,0:T(8,128)(2,1)S(1)}, bf16[256,2048]{1,0:T(8,128)(2,1)}, u32[]{:S(2)}) copy-start(bf16[256,2048]{1,0:T(8,128)(2,1)} %param.11) | copy-start | bytes 3145732
  132.9 18.8 %all-to-all-start.2 = ((bf16[32,1,1,4,2048]{4,3,2,1,0:T(4,128)(2,1)}), bf16[32,1,1,4,2048]{4,3,2,1,0:T(4,128)(2,1)}, u32[]{:S(2)}, u32[]{:S(2)}) async-start(bf16[32,1,1,4,2048]{4,3,2,1,0:T(4,128)(2,1)} %bitcast.89), calls=%async_computation.3 | async-start | bytes 1048576 | tf_op jit(solution)/shard_map/all_to_all | solution.py:27
  140.5 70.1 %all-gather.6.cloned.1.call-start = ((), (), s32[]{:S(2)}) async-start(), calls=%async_computation.6 | async-start | bytes 5242880 | tf_op jit(solution)/shard_map/all_gather | solution.py:130
  156.1 58.4 %copy-start.1 = (bf16[256,2048]{1,0:T(8,128)(2,1)}, bf16[256,2048]{1,0:T(8,128)(2,1)S(1)}, u32[]{:S(2)}) copy-start(bf16[256,2048]{1,0:T(8,128)(2,1)S(1)} %scatter_fusion) | copy-start | bytes 3145732
  164.6 102.8 %all-gather.8.cloned.1.call-start = ((), (), s32[]{:S(2)}) async-start(), calls=%async_computation.7 | async-start | bytes 4325376 | tf_op jit(solution)/shard_map/all_gather | solution.py:35
  210.6 4.2 %copy-start.3 = (bf16[256,8192]{1,0:T(8,128)(2,1)S(1)}, bf16[256,8192]{1,0:T(8,128)(2,1)}, u32[]{:S(2)}) copy-start(bf16[256,8192]{1,0:T(8,128)(2,1)} %all-gather.6.cloned.1.call-done) | copy-start | bytes 12582916
  210.6 4.2 %copy-start.4 = (bf16[8192,128]{1,0:T(8,128)(2,1)S(1)}, bf16[8192,128]{1,0:T(8,128)(2,1)}, u32[]{:S(2)}) copy-start(bf16[8192,128]{1,0:T(8,128)(2,1)} %param.15) | copy-start | bytes 6291460
Sparse Core Ops, SparseCore 0:
  10.3 51.1 all-gather.3
  100.2 27.7 reduce-scatter.1
  164.7 45.8 all-gather.5
  217.1 50.1 all-gather.7
where the time goes:
time: 348 us
  waiting for transfers between devices  167 us (48%)
  matrix products  69.8 us (20%)
  blocking collectives  39.7 us (11%)
  other arithmetic  30.1 us (9%)
  local copies, waits for them, and re-layouts  14.2 us (4%)
  between operations  14.1 us (4%)
  starting transfers between devices  12.9 us (4%)
    all_gather x1, waiting for transfers between devices, project_strips(): lax.all_gather(merger_hidden, ('role', 'seq'), axis=0, tiled=True)  53.5 us
    all_gather x1, waiting for transfers between devices, body(): shard_piece = lax.all_gather(normed, 'tp', axis=1, tiled=True)  45.9 us
    all_gather x1, waiting for transfers between devices, sent_together(): filled = lax.all_gather(both, axis, axis=dim, tiled=True)  36.6 us
    all_to_all x1, blocking collectives, body(): lax.all_to_all(strips, ('role', 'seq'), split_axis=0, concat_axis=1, tile...  32.9 us
    dot_general x1, matrix products, body(): jnp.einsum('qhgd,khd->hgqk', queries, key_piece, preferred_element_type=j...  25.4 us
    dot_general x1, matrix products, body(): jnp.einsum('hgqk,khd->hgqd', probability.astype(jnp.bfloat16), value_piec...  25.3 us
    reduce_sum x1, other arithmetic, body(): running_sum = jnp.sum(probability, axis=3)  22.3 us
    reduce_scatter x1, waiting for transfers between devices, sum_hidden(): lax.psum_scatter(partial_value, 'tp', scatter_dimension=1, tiled=True)  19.6 us
  transfers between devices with their start and end apart: 6, of which 5 were waited for; matrix products, arithmetic and copies ran while one was open for 6% of the time, Pallas kernels for 0%

commit v1 on v0

--- a/solution.py
+++ b/solution.py
@@ -5,6 +5,11 @@
 from jax.sharding import PartitionSpec as P
 
 HEAD_DIM = 128
+
+
+def exchange_gather(shard, axis, dim):
+    sent = jnp.stack([shard] * lax.axis_size(axis))
+    return jnp.concatenate(lax.all_to_all(sent, axis, 0, 0), axis=dim)
 
 
 def split_up(x, dim, length):
@@ -61,7 +66,7 @@
 
 def project_strips(merger_hidden, merger_out):
     return jnp.dot(
-        lax.all_gather(merger_hidden, ("role", "seq"), axis=0, tiled=True),
+        exchange_gather(merger_hidden, ("role", "seq"), 0),
         merger_out,
         preferred_element_type=jnp.float32,
     )

time: 348 us -> 363 us (1.043)
  blocking collectives: 39.7 us -> 110 us
  waiting for transfers between devices: 167 us -> 113 us
    all_to_all x0 -> x1, blocking collectives: none -> 70.8 us  [exchange_gather(): return jnp.concatenate(lax.all_to_all(sent, axis, 0, 0), axis=dim)]
    all_gather x1 -> x0, waiting for transfers between devices: 53.5 us -> none  [project_strips(): lax.all_gather(merger_hidden, ('role', 'seq'), axis=0, tiled=True)]
  transfers between devices with their start and end apart: 6 -> 5, of which waited for: 5 -> 4; matrix products, arithmetic and copies ran while one was open for 6% -> 6% of each run, Pallas kernels for 0% -> 0%
where the time goes in v1:
time: 363 us
  waiting for transfers between devices  113 us (31%)
  blocking collectives  110 us (30%)
  matrix products  67.2 us (19%)
  other arithmetic  30.1 us (8%)
  local copies, waits for them, and re-layouts  15.9 us (4%)
  between operations  14.1 us (4%)
  starting transfers between devices  13 us (4%)
    all_to_all x1, blocking collectives, exchange_gather(): return jnp.concatenate(lax.all_to_all(sent, axis, 0, 0), axis=dim)  70.8 us
    all_gather x1, waiting for transfers between devices, body(): shard_piece = lax.all_gather(normed, 'tp', axis=1, tiled=True)  45.8 us
    all_gather x1, waiting for transfers between devices, sent_together(): filled = lax.all_gather(both, axis, axis=dim, tiled=True)  36.6 us
    all_to_all x1, blocking collectives, body(): lax.all_to_all(strips, ('role', 'seq'), split_axis=0, concat_axis=1, tile...  32 us
    dot_general x1, matrix products, body(): jnp.einsum('qhgd,khd->hgqk', queries, key_piece, preferred_element_type=j...  25.4 us
    dot_general x1, matrix products, body(): jnp.einsum('hgqk,khd->hgqd', probability.astype(jnp.bfloat16), value_piec...  25.4 us
    reduce_sum x1, other arithmetic, body(): running_sum = jnp.sum(probability, axis=3)  22.3 us
    reduce_scatter x1, waiting for transfers between devices, sum_hidden(): lax.psum_scatter(partial_value, 'tp', scatter_dimension=1, tiled=True)  19.9 us
  transfers between devices with their start and end apart: 5, of which 4 were waited for; matrix products, arithmetic and copies ran while one was open for 6% of the time, Pallas kernels for 0%

profile of v1, /device:TPU:1, one launch (start us, length us, event | category | flops | bytes accessed | tf_op | source)
XLA Modules:
  0.0 362.9 jit_solution(14864263121105532357)
XLA Ops:
  7.2 0.0 reduce-scatter.2.cloned.1.call-start
  7.2 1.6 stack.2
  8.9 70.8 %all_to_all.31 = bf16[32,64,1280]{2,1,0:T(8,128)(2,1)S(1)} all-to-all(bf16[32,64,1280]{2,1,0:T(8,128)(2,1)S(1)} %stack.2), channel_id=1, replica_groups=mesh['role'=2,'seq'=16,'tp'=4] {'role','seq'}, dimensions={0} | all-to-all | bytes 10485760 | tf_op jit(solution)/shard_map/all_to_all | solution.py:12
  79.7 1.6 fusion.14
  81.3 32.0 %all_to_all.32 = f32[32,64,256]{2,1,0:T(8,128)S(1)} all-to-all(f32[32,64,256]{2,1,0:T(8,128)S(1)} %fusion.14), channel_id=1, replica_groups=mesh['role'=2,'seq'=16,'tp'=4] {'role','seq'}, dimensions={0} | all-to-all | bytes 4194304 | tf_op jit(solution)/shard_map/all_to_all | solution.py:93
  113.3 1.5 copy.48
  114.9 0.0 reduce-scatter.2.cloned.1.call-update
  114.9 0.1 fusion.27
  115.0 0.1 reduce_window_sum.11
  115.1 0.2 select_reduce_fusion
  115.3 0.8 scatter_custom_fusion
  116.1 0.1 pad_add_fusion
  116.2 1.2 gather_fusion
  117.4 0.7 reshape_transpose_transpose_reshape_reshape_reshape_reshape.6
  118.1 5.0 %all-to-all-start = ((s32[32,1,1,4]{3,2,1,0:T(1,128)}), s32[32,1,1,4]{3,2,1,0:T(1,128)S(1)}, u32[]{:S(2)}, u32[]{:S(2)}) async-start(s32[32,1,1,4]{3,2,1,0:T(1,128)} %bitcast), calls=%async_computation | async-start | bytes 32768 | tf_op jit(solution)/shard_map/all_to_all | solution.py:32
  123.1 19.9 %reduce-scatter.2.cloned.1.call-done = f32[64,2048]{1,0:T(8,128)} async-done(((f32[64,8192]{1,0:T(8,128)}), f32[64,2048]{1,0:T(8,128)}) %reduce-scatter.2.cloned.1.call-update) | async-done | bytes 524304 | tf_op jit(solution)/shard_map/reduce_scatter | solution.py:62
  143.0 1.1 convert_element_type.54
  144.1 1.7 gather_fusion.1
  145.8 2.0 reshape_transpose_transpose_reshape_reshape_reshape_reshape.7
  147.8 7.7 %all-to-all-start.3 = ((bf16[32,1,1,4,2048]{4,3,2,1,0:T(4,128)(2,1)}), bf16[32,1,1,4,2048]{4,3,2,1,0:T(4,128)(2,1)}, u32[]{:S(2)}, u32[]{:S(2)}) async-start(bf16[32,1,1,4,2048]{4,3,2,1,0:T(4,128)(2,1)} %bitcast.89), calls=%async_computation.4 | async-start | bytes 1048576 | tf_op jit(solution)/shard_map/all_to_all | solution.py:32
  155.5 0.0 all-gather.3.cloned.1.call-start
  155.6 0.1 copy.44
  155.7 0.1 copy.32
  155.8 0.1 select_n.64
  155.9 10.7 %all-to-all-done.3 = bf16[32,1,1,4,2048]{4,3,2,1,0:T(4,128)(2,1)} async-done(((bf16[32,1,1,4,2048]{4,3,2,1,0:T(4,128)(2,1)}), bf16[32,1,1,4,2048]{4,3,2,1,0:T(4,128)(2,1)}, u32[]{:S(2)}, u32[]{:S(2)}) %all-to-all-start.3) | async-done | bytes 524320 | tf_op jit(solution)/shard_map/all_to_all | solution.py:32
  166.7 2.0 reshape.306
  168.6 2.4 scatter_fusion
  171.1 0.3 fusion.7
  171.4 6.9 %psum.7 = f32[256]{0:T(256)S(1)} all-reduce(f32[256]{0:T(256)S(1)} %fusion.7), channel_id=1, replica_groups=mesh['role'=2,'seq'=16,'tp'=4] {'tp'}, use_global_device_ids=true, to_apply=%region_6.7 | all-reduce | flops 256 | bytes 2048 | tf_op jit(solution)/shard_map/psum | solution.py:131
  178.3 1.3 fusion.9
  179.5 0.0 all-gather.3.cloned.1.call-update
  179.6 0.2 all-gather.5.cloned.1.call-start
  179.8 45.8 %all-gather.3.cloned.1.call-done = bf16[256,8192]{1,0:T(8,128)(2,1)} async-done(((bf16[256,2048]{1,0:T(8,128)(2,1)}), bf16[256,8192]{1,0:T(8,128)(2,1)}) %all-gather.3.cloned.1.call-update) | async-done | bytes 4194320 | tf_op jit(solution)/shard_map/all_gather | solution.py:135
  225.6 3.8 %convolution_bitcast_fusion.1 = f32[256,1,128]{0,2,1:T(8,128)S(1)} fusion(bf16[256,8192]{1,0:T(8,128)(2,1)} %all-gather.3.cloned.1.call-done, bf16[8192,128]{1,0:T(8,128)(2,1)S(1)} %copy-done), kind=kOutput, calls=%fused_computation.22 | convolution fusion | flops 536870912 | bytes 6422528 | tf_op jit(solution)/shard_map/dot_general | solution.py:137
  229.4 0.3 fusion.24
  229.8 1.5 fusion.11
  231.3 0.7 pad_maximum_fusion
  232.0 0.5 multiply_cosine_fusion
  232.6 2.7 iota_compare_fusion
  235.3 9.5 %convolution_bitcast_fusion = f32[32,8,8,128]{3,1,2,0:T(8,128)S(1)} fusion(bf16[256,8192]{1,0:T(8,128)(2,1)} %all-gather.3.cloned.1.call-done, bf16[8192,1024]{1,0:T(8,128)(2,1)} %param.13), kind=kOutput, calls=%fused_computation.21 | convolution fusion | flops 4294967296 | bytes 22020096 | tf_op jit(solution)/shard_map/dot_general | solution.py:137
  244.8 0.2 copy.49
  245.0 0.3 fusion.36
  245.3 0.4 subtract_convert_fusion
  245.7 36.6 %all-gather.5.cloned.1.call-done = bf16[8192,2,128]{0,2,1:T(8,128)(2,1)} async-done(((bf16[256,2,128]{0,2,1:T(8,128)(2,1)}), bf16[8192,2,128]{0,2,1:T(8,128)(2,1)}) %all-gather.5.cloned.1.call-update) | async-done | bytes 4194320 | tf_op jit(solution)/shard_map/all_gather | solution.py:40
  282.3 25.4 %fusion = (f32[8,256]{1,0:T(8,128)S(1)}, f32[8192,256,8]{1,0,2:T(8,128)}) fusion(pred[256,8192]{0,1:T(8,128)(4,1)} %iota_compare_fusion, bf16[256,8,64]{2,0,1:T(8,128)(2,1)S(1)} %get-tuple-element.9, bf16[256,8,64]{2,0,1:T(8,128)(2,1)S(1)} %get-tuple-element.8, bf16[8192,2,128]{0,2,1:T(8,128)(2,1)} %all-gather.5.cloned.1.call-done), kind=kOutput, calls=%fused_computation.6 | convolution fusion | flops 4346345472 | bytes 71835648 | tf_op jit(solution)/shard_map/qhgd,khd->hgqk/dot_general | solution.py:155
  307.7 22.3 %fusion.1 = f32[8,256]{1,0:T(8,128)S(1)} fusion(f32[8192,256,8]{1,0,2:T(8,128)} %get-tuple-element.17, f32[8,256]{1,0:T(8,128)S(1)} %broadcast_maximum_fusion, pred[256,8192]{0,1:T(8,128)(4,1)} %iota_compare_fusion), kind=kLoop, calls=%fused_computation.7 | loop fusion | flops 83884032 | bytes 69222400 | tf_op jit(solution)/shard_map/reduce_sum | solution.py:163
  330.0 25.4 %divide_convert_fusion = bf16[8,256,128]{1,2,0:T(8,128)(2,1)S(1)} fusion(f32[8192,256,8]{1,0,2:T(8,128)} %get-tuple-element.17, f32[8,256]{1,0:T(8,128)S(1)} %broadcast_maximum_fusion, pred[256,8192]{0,1:T(8,128)(4,1)} %iota_compare_fusion, bf16[8192,2,128]{0,2,1:T(8,128)(2,1)} %all-gather.5.cloned.1.call-done, f32[8,256]{1,0:T(8,128)S(1)} %fusion.1), kind=kOutput, calls=%fused_computation.25 | convolution fusion | flops 4379377664 | bytes 71843840 | tf_op jit(solution)/shard_map/hgqk,khd->hgqd/dot_general | solution.py:164
  355.4 1.0 copy.40
  (33 shorter events, 0.2 us)
Async XLA Ops:
  7.2 218.4 %copy-start = (bf16[8192,128]{1,0:T(8,128)(2,1)S(1)}, bf16[8192,128]{1,0:T(8,128)(2,1)}, u32[]{:S(2)}) copy-start(bf16[8192,128]{1,0:T(8,128)(2,1)} %param.14) | copy-start | bytes 6291460
  7.2 135.8 %reduce-scatter.2.cloned.1.call-start = ((), (), s32[]{:S(2)}) async-start(), calls=%async_computation.5 | async-start | bytes 2621440 | tf_op jit(solution)/shard_map/reduce_scatter | solution.py:62
  8.9 70.9 %copy-start.6 = (bf16[1280,256]{1,0:T(8,128)(2,1)S(1)}, bf16[1280,256]{1,0:T(8,128)(2,1)}, u32[]{:S(2)}) copy-start(bf16[1280,256]{1,0:T(8,128)(2,1)} %param.9) | copy-start | bytes 1966084
  113.3 1.5 copy-start.7
  117.4 38.2 %copy-start.5 = (bf16[2048]{0:T(1024)(128)(2,1)S(1)}, bf16[2048]{0:T(1024)(128)(2,1)}, u32[]{:S(2)}) copy-start(bf16[2048]{0:T(1024)(128)(2,1)} %param.12) | copy-start | bytes 12292
  118.1 29.7 %all-to-all-start = ((s32[32,1,1,4]{3,2,1,0:T(1,128)}), s32[32,1,1,4]{3,2,1,0:T(1,128)S(1)}, u32[]{:S(2)}, u32[]{:S(2)}) async-start(s32[32,1,1,4]{3,2,1,0:T(1,128)} %bitcast), calls=%async_computation | async-start | bytes 32768 | tf_op jit(solution)/shard_map/all_to_all | solution.py:32
  144.0 24.6 %copy-start.2 = (bf16[256,2048]{1,0:T(8,128)(2,1)S(1)}, bf16[256,2048]{1,0:T(8,128)(2,1)}, u32[]{:S(2)}) copy-start(bf16[256,2048]{1,0:T(8,128)(2,1)} %param.11) | copy-start | bytes 3145732
  147.8 18.8 %all-to-all-start.3 = ((bf16[32,1,1,4,2048]{4,3,2,1,0:T(4,128)(2,1)}), bf16[32,1,1,4,2048]{4,3,2,1,0:T(4,128)(2,1)}, u32[]{:S(2)}, u32[]{:S(2)}) async-start(bf16[32,1,1,4,2048]{4,3,2,1,0:T(4,128)(2,1)} %bitcast.89), calls=%async_computation.4 | async-start | bytes 1048576 | tf_op jit(solution)/shard_map/all_to_all | solution.py:32
  155.5 70.1 %all-gather.3.cloned.1.call-start = ((), (), s32[]{:S(2)}) async-start(), calls=%async_computation.6 | async-start | bytes 5242880 | tf_op jit(solution)/shard_map/all_gather | solution.py:135
  171.1 58.4 %copy-start.1 = (bf16[256,2048]{1,0:T(8,128)(2,1)}, bf16[256,2048]{1,0:T(8,128)(2,1)S(1)}, u32[]{:S(2)}) copy-start(bf16[256,2048]{1,0:T(8,128)(2,1)S(1)} %scatter_fusion) | copy-start | bytes 3145732
  179.6 102.8 %all-gather.5.cloned.1.call-start = ((), (), s32[]{:S(2)}) async-start(), calls=%async_computation.7 | async-start | bytes 4325376 | tf_op jit(solution)/shard_map/all_gather | solution.py:40
  225.6 4.2 %copy-start.3 = (bf16[256,8192]{1,0:T(8,128)(2,1)S(1)}, bf16[256,8192]{1,0:T(8,128)(2,1)}, u32[]{:S(2)}) copy-start(bf16[256,8192]{1,0:T(8,128)(2,1)} %all-gather.3.cloned.1.call-done) | copy-start | bytes 12582916
  225.6 4.2 %copy-start.4 = (bf16[8192,128]{1,0:T(8,128)(2,1)S(1)}, bf16[8192,128]{1,0:T(8,128)(2,1)}, u32[]{:S(2)}) copy-start(bf16[8192,128]{1,0:T(8,128)(2,1)} %param.15) | copy-start | bytes 6291460
Sparse Core Ops, SparseCore 0:
  115.0 27.9 reduce-scatter.1
  179.7 45.8 all-gather.2
  232.1 50.1 all-gather.4
